TPU v7x, 32 devices: a whole 2x2x4 slice. The times are simulated.
32 devices in a mesh: leaf: 4 (over y, x), col: 8 (over z, core).
Axes of the slice: x: 2, y: 2, z: 4, core: 2. Of those that a mesh axis runs over, the one named last changes fastest.
Arguments:
- s_blocks: bfloat16 [64, 8, 128, 128], P(('leaf', 'col')), may hold values from -0.0059814453 to 0.0059814453
- z_blocks: bfloat16 [64, 8, 128, 128], P(('leaf', 'col')), may hold values from -1.5 to 1.5
- s_requests: int32 [4, 8, 8, 1], P('leaf', 'col'), may hold values from -1 to 15, as said below
- y_pairs: int32 [64, 8, 8], P(('leaf', 'col')), may hold values from -1 to 7, as said below
- zt_requests: int32 [4, 8, 8, 1], P('leaf', 'col'), may hold values from -1 to 31, as said below
- d_pairs: int32 [64, 8, 8], P(('leaf', 'col')), may hold values from -1 to 7, as said below
- d_requests: int32 [4, 8, 8, 1], P('leaf', 'col'), may hold values from -1 to 31, as said below
- e_pairs: int32 [64, 8, 8], P(('leaf', 'col')), may hold values from -1 to 7, as said below
- z_requests: int32 [4, 8, 8, 1], P('leaf', 'col'), may hold values from -1 to 31, as said below
- z_pairs: int32 [64, 8, 8], P(('leaf', 'col')), may hold values from -1 to 7, as said below
Outputs:
- z_refined: bfloat16 [64, 8, 128, 128], P(('leaf', 'col'))
Inputs may be any that keep to these rules, and one draw needn't show every extreme that they name: `s_requests`: entry [l, c, p, q] is -1 or a slot of the S holdings of the device (l, p); the entries of one [l, c, p] are distinct. Every reader has some peer with all 1 entries used, and one reader uses all entries. `zt_requests`: entry [l, c, p, q] is -1 or a slot of the Z holdings of the device (l, p); the entries of one [l, c, p] are distinct. Every reader has some peer with all 1 entries used, and one reader uses all entries. `d_requests`: entry [l, c, p, q] is -1 or a slot of the D holdings of the device (l, p); the entries of one [l, c, p] are distinct. Every reader has some peer with all 1 entries used, and one reader uses all entries. `z_requests`: entry [l, c, p, q] is -1 or a slot of the Z holdings of the device (l, p); the entries of one [l, c, p] are distinct. Every reader has some peer with all 1 entries used, and one reader uses all entries. `y_pairs`: each entry is -1 or the position p + q of an entry of s_requests that is not -1, for the reader holding the column; every such entry is named at least once. `d_pairs`: each entry is -1 or the position p + q of an entry of zt_requests that is not -1, for the reader holding the column; every such entry is named at least once. `e_pairs`: each entry is -1 or the position p + q of an entry of d_requests that is not -1, for the reader holding the column; every such entry is named at least once. `z_pairs`: each entry is -1 or the position p + q of an entry of z_requests that is not -1, for the reader holding the column; every such entry is named at least once.
All inputs are finite; a program needn't handle non-finite values.
Results may differ from a plain program's by a relative error of at most 0.0059.
Values may be sent and summed in bfloat16 or wider, within the bound.
A program may use at most 64 MiB of HBM per device.

v0:
```python
import jax
import jax.numpy as jnp
from jax import lax
from jax.sharding import PartitionSpec as P


def from_partner(value, axis, apart):
    mask = 2**apart
    pairs = [(source, source ^ mask) for source in range(lax.axis_size(axis))]
    return lax.ppermute(value, axis, pairs)


def pick_blocks(holdings, requests):
    lookup = jnp.maximum(requests, 0)
    blocks = jnp.take(holdings, lookup, axis=0)
    return jnp.where((requests >= 0)[:, :, None, None], blocks, jnp.zeros_like(blocks))


def fetch_blocks(holdings, requests):
    fetched = lax.all_to_all(
        pick_blocks(
            holdings, lax.all_to_all(requests, "col", split_axis=0, concat_axis=0, tiled=True)
        ),
        "col",
        split_axis=0,
        concat_axis=0,
        tiled=True,
    )
    return fetched.reshape((-1,) + holdings.shape[1:])


def block_products(fetched, pair_ids, local_blocks, flipped):
    fetch_count = fetched.shape[0]
    padded = jnp.concatenate([fetched, jnp.zeros((1,) + fetched.shape[1:], fetched.dtype)], axis=0)
    lookup = jnp.where(pair_ids < 0, fetch_count, pair_ids)
    chosen = jnp.take(padded, lookup, axis=0)
    einsum_form = "gabji,gbjk->gaik" if flipped else "gabij,gbjk->gaik"
    return jnp.einsum(einsum_form, chosen, local_blocks, preferred_element_type=jnp.float32)


def on_device(
    s_blocks,
    z_blocks,
    s_requests,
    y_pairs,
    zt_requests,
    d_pairs,
    d_requests,
    e_pairs,
    z_requests,
    z_pairs,
):
    columns, slot_count, block_size = (z_blocks.shape[0], z_blocks.shape[1], z_blocks.shape[2])
    flat_shape = (columns * slot_count, block_size, block_size)
    ask_shape = (s_requests.shape[2], s_requests.shape[3])
    s_asks = s_requests.reshape(ask_shape)
    zt_asks = zt_requests.reshape(ask_shape)
    d_asks = d_requests.reshape(ask_shape)
    z_asks = z_requests.reshape(ask_shape)
    s_own = s_blocks.reshape(flat_shape)
    z_own = z_blocks.reshape(flat_shape)
    z_holdings = jnp.concatenate([z_own, from_partner(z_own, "leaf", 0)], axis=0)
    s_fetched = fetch_blocks(s_own, s_asks)
    zt_fetched = fetch_blocks(z_holdings, zt_asks)
    y_blocks = block_products(s_fetched, y_pairs, z_blocks, False).astype(jnp.bfloat16)
    first_slot = (jnp.arange(slot_count) == 0).astype(jnp.float32)
    identity = first_slot[:, None, None] * jnp.eye(block_size, dtype=jnp.float32)
    d_blocks = (identity - block_products(zt_fetched, d_pairs, y_blocks, True)).astype(jnp.bfloat16)
    d_own = d_blocks.reshape(flat_shape)
    d_holdings = jnp.concatenate([d_own, from_partner(d_own, "leaf", 0)], axis=0)
    d_fetched = fetch_blocks(d_holdings, d_asks)
    z_fetched = fetch_blocks(z_holdings, z_asks)
    square = block_products(d_fetched, e_pairs, d_blocks, False)
    e_blocks = (0.5 * d_blocks.astype(jnp.float32) + 0.375 * square).astype(jnp.bfloat16)
    refined = z_blocks.astype(jnp.float32) + block_products(z_fetched, z_pairs, e_blocks, False)
    return refined.astype(jnp.bfloat16)


def solution(mesh):
    in_specs = (
        P(("leaf", "col"), None, None, None),
        P(("leaf", "col"), None, None, None),
        P("leaf", "col", None, None),
        P(("leaf", "col"), None, None),
        P("leaf", "col", None, None),
        P(("leaf", "col"), None, None),
        P("leaf", "col", None, None),
        P(("leaf", "col"), None, None),
        P("leaf", "col", None, None),
        P(("leaf", "col"), None, None),
    )
    out_specs = P(("leaf", "col"), None, None, None)
    return jax.shard_map(
        on_device, mesh=mesh, in_specs=in_specs, out_specs=out_specs, check_vma=False
    )
```

profile of v0, /device:TPU:0, one launch (start us, length us, event | category | flops | bytes accessed | tf_op | source)
XLA Modules:
  0.0 123.8 jit_solution(10315109005999071094)
XLA Ops:
  0.0 3.0 %collective-permute-start = (bf16[16,128,128]{2,1,0:T(8,128)(2,1)}, bf16[16,128,128]{2,1,0:T(8,128)(2,1)S(1)}, u32[]{:S(2)}, u32[]{:S(2)}) collective-permute-start(bf16[16,128,128]{2,1,0:T(8,128)(2,1)} %bitcast.130), channel_id=1, source_target_pairs={{0,8},{8,0},{16,24},{24,16},{1,9},{9,1},{17,25},{25,17},{2,10},{10... | collective-permute-start | bytes 1572872 | tf_op jit(solution)/shard_map/ppermute | solution.py:10
  3.0 1.3 %copy.18 = s32[8,1,1]{2,1,0:T(1,128)} copy(s32[8,1,1]{0,2,1:T(1,128)} %bitcast.134) | data formatting | bytes 64 | tf_op jit(solution)/shard_map/all_to_all | solution.py:22
  4.3 4.9 %all-to-all-start.2 = ((s32[8,1,1]{2,1,0:T(1,128)}), s32[8,1,1]{2,1,0:T(1,128)S(1)}, u32[]{:S(2)}, u32[]{:S(2)}) async-start(s32[8,1,1]{2,1,0:T(1,128)} %copy.18), calls=%async_computation.2 | async-start | bytes 8192 | tf_op jit(solution)/shard_map/all_to_all | solution.py:22
  9.2 0.7 compare_select_fusion.2
  9.9 0.7 compare_select_fusion.1
  10.6 0.7 compare_and_fusion.1
  11.3 0.1 reshape.282
  11.4 1.3 %copy.20 = s32[8,1,1]{2,1,0:T(1,128)} copy(s32[8,1,1]{0,2,1:T(1,128)} %bitcast.135) | data formatting | bytes 64 | tf_op jit(solution)/shard_map/all_to_all | solution.py:22
  12.7 0.1 reshape.286
  12.8 1.3 %copy.21 = s32[8,1,1]{2,1,0:T(1,128)} copy(s32[8,1,1]{0,2,1:T(1,128)} %bitcast.136) | data formatting | bytes 64 | tf_op jit(solution)/shard_map/all_to_all | solution.py:22
  14.2 0.7 compare_select_fusion
  14.9 0.1 broadcast_multiply_fusion
  15.0 1.3 %copy.17 = s32[8,1,1]{2,1,0:T(1,128)} copy(s32[8,1,1]{0,2,1:T(1,128)} %bitcast.137) | data formatting | bytes 64 | tf_op jit(solution)/shard_map/all_to_all | solution.py:22
  16.3 0.0 all-to-all-done.2
  16.3 5.1 %all-to-all-start.4 = ((s32[8,1,1]{2,1,0:T(1,128)}), s32[8,1,1]{2,1,0:T(1,128)S(1)}, u32[]{:S(2)}, u32[]{:S(2)}) async-start(s32[8,1,1]{2,1,0:T(1,128)} %copy.20), calls=%async_computation.4 | async-start | bytes 8192 | tf_op jit(solution)/shard_map/all_to_all | solution.py:22
  21.4 0.2 maximum_reduce_fusion.1
  21.6 5.3 %all-to-all-done.4 = s32[8,1,1]{2,1,0:T(1,128)S(1)} async-done(((s32[8,1,1]{2,1,0:T(1,128)}), s32[8,1,1]{2,1,0:T(1,128)S(1)}, u32[]{:S(2)}, u32[]{:S(2)}) %all-to-all-start.4) | async-done | bytes 64 | tf_op jit(solution)/shard_map/all_to_all | solution.py:22
  27.0 3.3 %all-to-all-start.6 = ((s32[8,1,1]{2,1,0:T(1,128)}), s32[8,1,1]{2,1,0:T(1,128)S(1)}, u32[]{:S(2)}, u32[]{:S(2)}) async-start(s32[8,1,1]{2,1,0:T(1,128)} %copy.21), calls=%async_computation.6 | async-start | bytes 8192 | tf_op jit(solution)/shard_map/all_to_all | solution.py:22
  30.3 0.2 maximum_reduce_fusion.3
  30.5 0.0 copy-done
  30.5 0.6 gather_fusion
  31.1 0.4 compare_reduce_fusion.2
  31.5 0.8 fusion.69
  32.3 0.2 compare_reduce_fusion.3
  32.6 3.2 %all-to-all-done.6 = s32[8,1,1]{2,1,0:T(1,128)S(1)} async-done(((s32[8,1,1]{2,1,0:T(1,128)}), s32[8,1,1]{2,1,0:T(1,128)S(1)}, u32[]{:S(2)}, u32[]{:S(2)}) %all-to-all-start.6) | async-done | bytes 64 | tf_op jit(solution)/shard_map/all_to_all | solution.py:22
  35.8 3.3 %all-to-all-start = ((s32[8,1,1]{2,1,0:T(1,128)}), s32[8,1,1]{2,1,0:T(1,128)S(1)}, u32[]{:S(2)}, u32[]{:S(2)}) async-start(s32[8,1,1]{2,1,0:T(1,128)} %copy.17), calls=%async_computation | async-start | bytes 8192 | tf_op jit(solution)/shard_map/all_to_all | solution.py:22
  39.1 0.2 maximum_reduce_fusion
  39.3 0.2 compare_reduce_fusion
  39.6 5.0 %all-to-all-done = s32[8,1,1]{2,1,0:T(1,128)S(1)} async-done(((s32[8,1,1]{2,1,0:T(1,128)}), s32[8,1,1]{2,1,0:T(1,128)S(1)}, u32[]{:S(2)}, u32[]{:S(2)}) %all-to-all-start) | async-done | bytes 64 | tf_op jit(solution)/shard_map/all_to_all | solution.py:22
  44.5 3.4 %all-to-all-start.5 = ((bf16[8,1,128,128]{3,2,1,0:T(8,128)(2,1)}), bf16[8,1,128,128]{3,2,1,0:T(8,128)(2,1)S(1)}, u32[]{:S(2)}, u32[]{:S(2)}) async-start(bf16[8,1,128,128]{3,2,1,0:T(8,128)(2,1)} %fusion.69), calls=%async_computation.5 | async-start | bytes 524288 | tf_op jit(solution)/shard_map/all_to_all | solution.py:20
  48.0 0.2 maximum_reduce_fusion.2
  48.2 0.2 compare_reduce_fusion.4
  48.5 0.0 collective-permute-done
  48.5 1.1 pad_maximum_fusion
  49.6 0.6 gather_fusion.3
  50.2 0.8 fusion.70
  51.0 6.6 %all-to-all-done.5 = bf16[8,1,128,128]{3,2,1,0:T(8,128)(2,1)S(1)} async-done(((bf16[8,1,128,128]{3,2,1,0:T(8,128)(2,1)}), bf16[8,1,128,128]{3,2,1,0:T(8,128)(2,1)S(1)}, u32[]{:S(2)}, u32[]{:S(2)}) %all-to-all-start.5) | async-done | bytes 262176 | tf_op jit(solution)/shard_map/all_to_all | solution.py:20
  57.6 3.4 %all-to-all-start.3 = ((bf16[8,1,128,128]{3,2,1,0:T(8,128)(2,1)}), bf16[8,1,128,128]{3,2,1,0:T(8,128)(2,1)S(1)}, u32[]{:S(2)}, u32[]{:S(2)}) async-start(bf16[8,1,128,128]{3,2,1,0:T(8,128)(2,1)} %fusion.70), calls=%async_computation.3 | async-start | bytes 524288 | tf_op jit(solution)/shard_map/all_to_all | solution.py:20
  61.1 3.0 %gather_fusion.5 = bf16[128,128,128]{2,1,0:T(8,128)(2,1)} fusion(bf16[9,128,128]{2,1,0:T(8,128)(2,1)S(1)} %concatenate.21, s32[1024]{0:T(1024)S(1)} %pad_clamp_fusion.2), kind=kCustom, calls=%fused_computation.5.clone | custom fusion | bytes 8389120 | tf_op jit(solution)/shard_map/jit(_take)/gather | solution.py:36
  64.1 6.5 %all-to-all-done.3 = bf16[8,1,128,128]{3,2,1,0:T(8,128)(2,1)S(1)} async-done(((bf16[8,1,128,128]{3,2,1,0:T(8,128)(2,1)}), bf16[8,1,128,128]{3,2,1,0:T(8,128)(2,1)S(1)}, u32[]{:S(2)}, u32[]{:S(2)}) %all-to-all-start.3) | async-done | bytes 262176 | tf_op jit(solution)/shard_map/all_to_all | solution.py:20
  70.7 3.1 %gather_fusion.4 = bf16[128,128,128]{2,1,0:T(8,128)(2,1)} fusion(bf16[9,128,128]{2,1,0:T(8,128)(2,1)S(1)} %concatenate.20, s32[1024]{0:T(1024)S(1)} %pad_clamp_fusion.4), kind=kCustom, calls=%fused_computation.4.clone | custom fusion | bytes 8389120 | tf_op jit(solution)/shard_map/jit(_take)/gather | solution.py:36
  73.7 6.3 %copy.19 = bf16[2,8,8,128,128]{3,4,2,1,0:T(8,128)(2,1)} copy(bf16[2,8,8,128,128]{4,3,2,1,0:T(8,128)(2,1)} %bitcast.122) | data formatting | bytes 8388608 | tf_op jit(solution)/shard_map/jit(_take)/gather | solution.py:36
  80.0 5.8 %fusion.49 = bf16[2,8,128,128]{3,2,1,0:T(8,128)(2,1)S(1)} fusion(bf16[2,8,8,128,128]{3,4,2,1,0:T(8,128)(2,1)} %copy.19, pred[2,8,8]{2,1,0:T(8,128)(4,1)S(1)} %get-tuple-element.10, bf16[2,8,8,128,128]{4,3,2,1,0:T(8,128)(2,1)} %bitcast.123, pred[2,8,8]{2,1,0:T(8,128)(4,1)S(1)} %get-tuple-element.9, bf16[2,8,128,128]{3,2,1,0:T(8,128)(2,1)S(1)} %copy-done.1, ...), kind=kOutput, calls=%fused_computation.35 | convolution fusion | flops 1078722560 | bytes 9961728 | tf_op jit(solution)/shard_map/gabji,gbjk->gaik/dot_general | solution.py:38
  85.9 0.0 copy-start.2
  85.9 0.0 copy-start.4
  85.9 0.0 copy-start.5
  85.9 0.6 collective-permute-start.1
  86.5 0.6 gather_fusion.1
  87.1 0.8 fusion.71
  87.9 3.4 %all-to-all-start.1 = ((bf16[8,1,128,128]{3,2,1,0:T(8,128)(2,1)}), bf16[8,1,128,128]{3,2,1,0:T(8,128)(2,1)S(1)}, u32[]{:S(2)}, u32[]{:S(2)}) async-start(bf16[8,1,128,128]{3,2,1,0:T(8,128)(2,1)} %fusion.71), calls=%async_computation.1 | async-start | bytes 524288 | tf_op jit(solution)/shard_map/all_to_all | solution.py:20
  91.4 7.9 %collective-permute-done.1 = bf16[16,128,128]{2,1,0:T(8,128)(2,1)S(1)} collective-permute-done((bf16[16,128,128]{2,1,0:T(8,128)(2,1)S(1)}, bf16[16,128,128]{2,1,0:T(8,128)(2,1)S(1)}, u32[]{:S(2)}, u32[]{:S(2)}) %collective-permute-start.1) | collective-permute-done | bytes 524320 | tf_op jit(solution)/shard_map/ppermute | solution.py:10
  99.3 0.1 pad_maximum_fusion.1
  99.4 0.6 gather_fusion.6
  100.0 0.8 fusion.68
  100.8 0.2 all-to-all-done.1
  101.0 3.4 %all-to-all-start.7 = ((bf16[8,1,128,128]{3,2,1,0:T(8,128)(2,1)}), bf16[8,1,128,128]{3,2,1,0:T(8,128)(2,1)S(1)}, u32[]{:S(2)}, u32[]{:S(2)}) async-start(bf16[8,1,128,128]{3,2,1,0:T(8,128)(2,1)} %fusion.68), calls=%async_computation.7 | async-start | bytes 524288 | tf_op jit(solution)/shard_map/all_to_all | solution.py:20
  104.4 0.1 reshape.294
  104.5 0.1 reshape.274
  104.7 3.0 %gather_fusion.2 = bf16[128,128,128]{2,1,0:T(8,128)(2,1)} fusion(bf16[9,128,128]{2,1,0:T(8,128)(2,1)S(1)} %concatenate.19, s32[1024]{0:T(1024)S(1)} %pad_clamp_fusion.6), kind=kCustom, calls=%fused_computation.1.clone | custom fusion | bytes 8389120 | tf_op jit(solution)/shard_map/jit(_take)/gather | solution.py:36
  107.7 6.3 %all-to-all-done.7 = bf16[8,1,128,128]{3,2,1,0:T(8,128)(2,1)S(1)} async-done(((bf16[8,1,128,128]{3,2,1,0:T(8,128)(2,1)}), bf16[8,1,128,128]{3,2,1,0:T(8,128)(2,1)S(1)}, u32[]{:S(2)}, u32[]{:S(2)}) %all-to-all-start.7) | async-done | bytes 262176 | tf_op jit(solution)/shard_map/all_to_all | solution.py:20
  114.1 0.0 copy-start.3
  114.1 3.0 %gather_fusion.7 = bf16[128,128,128]{2,1,0:T(8,128)(2,1)} fusion(bf16[9,128,128]{2,1,0:T(8,128)(2,1)S(1)} %concatenate.23, s32[1024]{0:T(1024)S(1)} %pad_clamp_fusion), kind=kCustom, calls=%fused_computation.6.clone | custom fusion | bytes 8389120 | tf_op jit(solution)/shard_map/jit(_take)/gather | solution.py:36
  117.1 0.0 copy-done.3
  117.1 6.6 %fusion.46 = bf16[2,8,128,128]{3,2,1,0:T(8,128)(2,1)} fusion(bf16[2,8,8,128,128]{4,3,2,1,0:T(8,128)(2,1)} %bitcast.124, pred[2,8,8]{2,1,0:T(8,128)(4,1)S(1)} %get-tuple-element.12, bf16[2,8,128,128]{3,2,1,0:T(8,128)(2,1)S(1)} %copy-done.1, bf16[2,8,8,128,128]{4,3,2,1,0:T(8,128)(2,1)} %bitcast.125, pred[2,8,8]{2,1,0:T(8,128)(4,1)S(1)} %get-tuple-element.11, ...), kind=kOutput, calls=%fused_computation.34 | convolution fusion | flops 1080033280 | bytes 9961728 | tf_op jit(solution)/shard_map/gabij,gbjk->gaik/dot_general | solution.py:38
  (28 shorter events, 0.2 us)
Async XLA Ops:
  0.0 30.5 %copy-start = (bf16[2,8,128,128]{3,2,1,0:T(8,128)(2,1)S(1)}, bf16[2,8,128,128]{3,2,1,0:T(8,128)(2,1)}, u32[]{:S(2)}) copy-start(bf16[2,8,128,128]{3,2,1,0:T(8,128)(2,1)} %param.14) | copy-start | bytes 1572868
  0.0 48.5 %collective-permute-start = (bf16[16,128,128]{2,1,0:T(8,128)(2,1)}, bf16[16,128,128]{2,1,0:T(8,128)(2,1)S(1)}, u32[]{:S(2)}, u32[]{:S(2)}) collective-permute-start(bf16[16,128,128]{2,1,0:T(8,128)(2,1)} %bitcast.130), channel_id=1, source_target_pairs={{0,8},{8,0},{16,24},{24,16},{1,9},{9,1},{17,25},{25,17},{2,10},{10... | collective-permute-start | bytes 1572872 | tf_op jit(solution)/shard_map/ppermute | solution.py:10
  4.3 12.0 %all-to-all-start.2 = ((s32[8,1,1]{2,1,0:T(1,128)}), s32[8,1,1]{2,1,0:T(1,128)S(1)}, u32[]{:S(2)}, u32[]{:S(2)}) async-start(s32[8,1,1]{2,1,0:T(1,128)} %copy.18), calls=%async_computation.2 | async-start | bytes 8192 | tf_op jit(solution)/shard_map/all_to_all | solution.py:22
  16.3 10.7 %all-to-all-start.4 = ((s32[8,1,1]{2,1,0:T(1,128)}), s32[8,1,1]{2,1,0:T(1,128)S(1)}, u32[]{:S(2)}, u32[]{:S(2)}) async-start(s32[8,1,1]{2,1,0:T(1,128)} %copy.20), calls=%async_computation.4 | async-start | bytes 8192 | tf_op jit(solution)/shard_map/all_to_all | solution.py:22
  27.0 8.8 %all-to-all-start.6 = ((s32[8,1,1]{2,1,0:T(1,128)}), s32[8,1,1]{2,1,0:T(1,128)S(1)}, u32[]{:S(2)}, u32[]{:S(2)}) async-start(s32[8,1,1]{2,1,0:T(1,128)} %copy.21), calls=%async_computation.6 | async-start | bytes 8192 | tf_op jit(solution)/shard_map/all_to_all | solution.py:22
  35.8 8.8 %all-to-all-start = ((s32[8,1,1]{2,1,0:T(1,128)}), s32[8,1,1]{2,1,0:T(1,128)S(1)}, u32[]{:S(2)}, u32[]{:S(2)}) async-start(s32[8,1,1]{2,1,0:T(1,128)} %copy.17), calls=%async_computation | async-start | bytes 8192 | tf_op jit(solution)/shard_map/all_to_all | solution.py:22
  44.5 13.1 %all-to-all-start.5 = ((bf16[8,1,128,128]{3,2,1,0:T(8,128)(2,1)}), bf16[8,1,128,128]{3,2,1,0:T(8,128)(2,1)S(1)}, u32[]{:S(2)}, u32[]{:S(2)}) async-start(bf16[8,1,128,128]{3,2,1,0:T(8,128)(2,1)} %fusion.69), calls=%async_computation.5 | async-start | bytes 524288 | tf_op jit(solution)/shard_map/all_to_all | solution.py:20
  57.6 13.1 %all-to-all-start.3 = ((bf16[8,1,128,128]{3,2,1,0:T(8,128)(2,1)}), bf16[8,1,128,128]{3,2,1,0:T(8,128)(2,1)S(1)}, u32[]{:S(2)}, u32[]{:S(2)}) async-start(bf16[8,1,128,128]{3,2,1,0:T(8,128)(2,1)} %fusion.70), calls=%async_computation.3 | async-start | bytes 524288 | tf_op jit(solution)/shard_map/all_to_all | solution.py:20
  73.7 6.3 %copy-start.1 = (bf16[2,8,128,128]{3,2,1,0:T(8,128)(2,1)S(1)}, bf16[2,8,128,128]{3,2,1,0:T(8,128)(2,1)}, u32[]{:S(2)}) copy-start(bf16[2,8,128,128]{3,2,1,0:T(8,128)(2,1)} %param.15) | copy-start | bytes 1572868
  85.9 13.4 %copy-start.2 = (bf16[2,8,128,128]{3,2,1,0:T(8,128)(2,1)}, bf16[2,8,128,128]{3,2,1,0:T(8,128)(2,1)S(1)}, u32[]{:S(2)}) copy-start(bf16[2,8,128,128]{3,2,1,0:T(8,128)(2,1)S(1)} %fusion.49) | copy-start | bytes 1572868
  85.9 18.5 %copy-start.4 = (s32[2,8,8]{2,1,0:T(8,128)S(1)}, s32[2,8,8]{2,1,0:T(8,128)}, u32[]{:S(2)}) copy-start(s32[2,8,8]{2,1,0:T(8,128)} %param.23) | copy-start | bytes 1540
  85.9 18.7 %copy-start.5 = (s32[2,8,8]{2,1,0:T(8,128)S(1)}, s32[2,8,8]{2,1,0:T(8,128)}, u32[]{:S(2)}) copy-start(s32[2,8,8]{2,1,0:T(8,128)} %param.21) | copy-start | bytes 1540
  85.9 13.4 %collective-permute-start.1 = (bf16[16,128,128]{2,1,0:T(8,128)(2,1)S(1)}, bf16[16,128,128]{2,1,0:T(8,128)(2,1)S(1)}, u32[]{:S(2)}, u32[]{:S(2)}) collective-permute-start(bf16[16,128,128]{2,1,0:T(8,128)(2,1)S(1)} %bitcast.132), channel_id=1, source_target_pairs={{0,8},{8,0},{16,24},{24,16},{1,9},{9,1},{17,25},{25,17},{2,10},{10... | collective-permute-start | bytes 1572872 | tf_op jit(solution)/shard_map/ppermute | solution.py:10
  87.9 13.1 %all-to-all-start.1 = ((bf16[8,1,128,128]{3,2,1,0:T(8,128)(2,1)}), bf16[8,1,128,128]{3,2,1,0:T(8,128)(2,1)S(1)}, u32[]{:S(2)}, u32[]{:S(2)}) async-start(bf16[8,1,128,128]{3,2,1,0:T(8,128)(2,1)} %fusion.71), calls=%async_computation.1 | async-start | bytes 524288 | tf_op jit(solution)/shard_map/all_to_all | solution.py:20
  101.0 13.1 %all-to-all-start.7 = ((bf16[8,1,128,128]{3,2,1,0:T(8,128)(2,1)}), bf16[8,1,128,128]{3,2,1,0:T(8,128)(2,1)S(1)}, u32[]{:S(2)}, u32[]{:S(2)}) async-start(bf16[8,1,128,128]{3,2,1,0:T(8,128)(2,1)} %fusion.68), calls=%async_computation.7 | async-start | bytes 524288 | tf_op jit(solution)/shard_map/all_to_all | solution.py:20
  114.1 3.1 %copy-start.3 = (bf16[2,8,128,128]{3,2,1,0:T(8,128)(2,1)S(1)}, bf16[2,8,128,128]{3,2,1,0:T(8,128)(2,1)}, u32[]{:S(2)}) copy-start(bf16[2,8,128,128]{3,2,1,0:T(8,128)(2,1)} %copy-done.2) | copy-start | bytes 1572868
where the time goes:
time: 125 us; the launch traced here: 124 us
  waiting for transfers between devices  41.1 us (33%)
  starting transfers between devices  33.8 us (27%)
  local copies, waits for them, and re-layouts  26.6 us (21%)
  matrix products  12.5 us (10%)
  other arithmetic  9.53 us (8%)
    all_to_all x4, waiting for transfers between devices, fetch_blocks(): lax.all_to_all(pick_blocks(holdings, lax.all_to_all(requests, 'col', spli...  19.6 us
    gather x5, local copies, waits for them, and re-layouts, block_products(): chosen = jnp.take(padded, lookup, axis=0)  18.4 us
    all_to_all x4, starting transfers between devices, fetch_blocks(): lax.all_to_all(requests, 'col', split_axis=0, concat_axis=0, tiled=True)  16.6 us
    all_to_all x4, starting transfers between devices, fetch_blocks(): lax.all_to_all(pick_blocks(holdings, lax.all_to_all(requests, 'col', spli...  13.6 us
    all_to_all x4, waiting for transfers between devices, fetch_blocks(): lax.all_to_all(requests, 'col', split_axis=0, concat_axis=0, tiled=True)  13.5 us
    dot_general x2, matrix products, block_products(): jnp.einsum(einsum_form, chosen, local_blocks, preferred_element_type=jnp....  12.5 us
    ppermute x2, waiting for transfers between devices, from_partner(): return lax.ppermute(value, axis, pairs)  7.92 us
    all_to_all x4, local copies, waits for them, and re-layouts, fetch_blocks(): lax.all_to_all(requests, 'col', split_axis=0, concat_axis=0, tiled=True)  5.28 us
  transfers between devices with their start and end apart: 10, of which 8 were waited for; matrix products, arithmetic and copies ran while one was open for 19% of the time, Pallas kernels for 0%

commit v1 on v0

v1 whole, which is shorter than its diff:
```python
import functools

import jax
import jax.numpy as jnp
from jax import lax
from jax.experimental import pallas as pl
from jax.experimental.pallas import tpu as pltpu
from jax.sharding import PartitionSpec as P

MESH = pl.DeviceIdType.MESH
S, T, Z, D = range(4)


def kernel(
    n,
    cap,
    cols,
    slots,
    req_ref,
    pairs_ref,
    s_ref,
    z_ref,
    out_ref,
    allreq,
    send_s,
    send_t,
    send_z,
    send_d,
    xs_t,
    xs_z,
    xs_d,
    xr_t,
    xr_z,
    xr_d,
    f_s,
    f_t,
    f_z,
    f_d,
    y_ref,
    d_ref,
    e_ref,
    req_send,
    req_recv,
    own_sem,
    z_send,
    z_recv,
    x_send,
    x_recv,
):
    leaf = lax.axis_index("leaf")
    me = lax.axis_index("col")
    partner = leaf + 1 - 2 * lax.rem(leaf, 2)
    hold = cols * slots
    size = z_ref.shape[1]
    fetch = n * cap
    sends = {S: send_s, T: send_t, Z: send_z, D: send_d}
    fetched = {S: f_s, T: f_t, Z: f_z, D: f_d}
    xsends = {T: xs_t, Z: xs_z, D: xs_d}
    xrecvs = {T: xr_t, Z: xr_z, D: xr_d}

    def loop(count, body):
        def step(k, carry):
            body(k)
            return carry

        lax.fori_loop(0, count, step, 0)

    def at(k):
        return lax.rem(me + k, n)

    barrier = pltpu.get_barrier_semaphore()

    def greet_own(k):
        pl.semaphore_signal(barrier, inc=1, device_id=(leaf, at(k + 1)), device_id_type=MESH)

    def greet_other(k):
        pl.semaphore_signal(barrier, inc=1, device_id=(partner, at(k)), device_id_type=MESH)

    loop(n - 1, greet_own)
    loop(n, greet_other)
    for f in (f_s, f_t, f_z, f_d):
        f[fetch] = jnp.zeros((size, size), f.dtype)
    own_copy = pltpu.make_async_copy(req_ref, allreq.at[me], own_sem)
    own_copy.start()
    pl.semaphore_wait(barrier, 2 * n - 1)

    def req_copy(side, to_leaf, to, source):
        return pltpu.make_async_remote_copy(
            src_ref=req_ref,
            dst_ref=allreq.at[side * n + source],
            send_sem=req_send.at[side * n + to],
            recv_sem=req_recv.at[side * n + source],
            device_id=(to_leaf, to),
            device_id_type=MESH,
        )

    loop(n - 1, lambda k: req_copy(0, leaf, at(k + 1), me).start())
    loop(n, lambda k: req_copy(1, partner, at(k), me).start())
    own_copy.wait()
    loop(n - 1, lambda k: req_copy(0, leaf, at(k + 1), at(k + 1)).wait_recv())
    loop(n, lambda k: req_copy(1, partner, at(k), at(k)).wait_recv())

    def ask(kind, side, c, q):
        word = kind * fetch + me * cap + q
        return allreq[side * n + c, lax.div(word, 128), lax.rem(word, 128)]

    def x_copy(kind, c):
        span = pl.ds(c * cap, cap)
        return pltpu.make_async_remote_copy(
            src_ref=xsends[kind].at[span],
            dst_ref=xrecvs[kind].at[span],
            send_sem=x_send.at[kind, c],
            recv_sem=x_recv.at[kind, c],
            device_id=(partner, me),
            device_id_type=MESH,
        )

    def z_copy(kind, to, source):
        return pltpu.make_async_remote_copy(
            src_ref=sends[kind].at[pl.ds(to * cap, cap)],
            dst_ref=fetched[kind].at[pl.ds(source * cap, cap)],
            send_sem=z_send.at[kind, to],
            recv_sem=z_recv.at[kind, source],
            device_id=(leaf, to),
            device_id_type=MESH,
        )

    def x_pass(kind, own_ref):
        def body(k):
            c = at(k)
            for q in range(cap):
                slot = jnp.clip(ask(kind, 1, c, q) - hold, 0, hold - 1)
                xsends[kind][c * cap + q] = own_ref[slot]
            x_copy(kind, c).start()

        return body

    def chosen(kind, own_ref, c, q):
        request = ask(kind, 0, c, q)
        block = own_ref[jnp.clip(request, 0, hold - 1)]
        if kind != S:
            block = jnp.where(request < hold, block, xrecvs[kind][c * cap + q])
        if kind == T:
            block = block.T
        return block

    def z_pass(kind, own_ref):
        def body(k):
            c = at(k + 1)
            if kind != S:
                x_copy(kind, c).wait_recv()
            for q in range(cap):
                sends[kind][c * cap + q] = chosen(kind, own_ref, c, q)
            z_copy(kind, c, me).start()

        loop(n - 1, body)
        if kind != S:
            x_copy(kind, me).wait_recv()
        for q in range(cap):
            fetched[kind][me * cap + q] = chosen(kind, own_ref, me, q)

    def arrived(kind):
        loop(n - 1, lambda k: z_copy(kind, at(k + 1), at(k + 1)).wait_recv())

    def x_order(k):
        return lax.rem(k + 1, n)

    def product(kind, base, local_ref, finish):
        f = fetched[kind]

        def body(a):
            for g in range(cols):
                row = base * cols * slots * slots + (g * slots + a) * slots
                blocks = []
                for b in range(slots):
                    name = pairs_ref[row + b]
                    blocks.append(f[jnp.where(name < 0, fetch, name)])
                lhs = jnp.concatenate(blocks, axis=1)
                rhs = local_ref[pl.ds(g * slots, slots)].reshape(slots * size, size)
                finish(g * slots + a, a, jnp.dot(lhs, rhs, preferred_element_type=jnp.float32))

        loop(slots, body)

    def x_start(kind, own_ref):
        body = x_pass(kind, own_ref)
        loop(n, lambda k: body(x_order(k)))

    z_pass(S, s_ref)
    x_start(T, z_ref)
    x_start(Z, z_ref)
    z_pass(T, z_ref)

    arrived(S)

    def y_finish(i, a, total):
        y_ref[i] = total.astype(y_ref.dtype)

    product(S, 0, z_ref, y_finish)
    z_pass(Z, z_ref)
    arrived(T)

    def d_finish(i, a, total):
        rows = lax.broadcasted_iota(jnp.int32, (size, size), 0)
        columns = lax.broadcasted_iota(jnp.int32, (size, size), 1)
        first = jnp.where(a == 0, 1.0, 0.0)
        d_ref[i] = (jnp.where(rows == columns, first, 0.0) - total).astype(d_ref.dtype)

    product(T, 1, y_ref, d_finish)
    x_start(D, d_ref)
    z_pass(D, d_ref)
    arrived(D)

    def e_finish(i, a, total):
        e_ref[i] = (0.5 * d_ref[i].astype(jnp.float32) + 0.375 * total).astype(e_ref.dtype)

    product(D, 2, d_ref, e_finish)
    arrived(Z)

    def z_finish(i, a, total):
        out_ref[i] = (z_ref[i].astype(jnp.float32) + total).astype(out_ref.dtype)

    product(Z, 3, e_ref, z_finish)

    loop(n - 1, lambda k: req_copy(0, leaf, at(k + 1), me).wait_send())
    loop(n, lambda k: req_copy(1, partner, at(k), me).wait_send())
    for kind in (S, T, Z, D):
        loop(n - 1, lambda k: z_copy(kind, at(k + 1), me).wait_send())
        if kind != S:
            loop(n, lambda k: x_copy(kind, k).wait_send())


def on_device(
    n,
    s_blocks,
    z_blocks,
    s_requests,
    y_pairs,
    zt_requests,
    d_pairs,
    d_requests,
    e_pairs,
    z_requests,
    z_pairs,
):
    cols, slots, size = z_blocks.shape[:3]
    cap = s_requests.shape[3]
    hold = cols * slots
    flat = (hold, size, size)
    fetch = n * cap
    requests = jnp.concatenate(
        [r.reshape(-1) for r in (s_requests, zt_requests, z_requests, d_requests)]
    )
    rows = pl.cdiv(requests.shape[0], 128)
    requests = jnp.pad(requests, (0, rows * 128 - requests.shape[0])).reshape(rows, 128)
    pairs = jnp.concatenate([p.reshape(-1) for p in (y_pairs, d_pairs, e_pairs, z_pairs)])
    kind = z_blocks.dtype

    def blocks(count):
        return pltpu.VMEM((count, size, size), kind)

    vmem = pl.BlockSpec(memory_space=pltpu.VMEM)
    smem = pl.BlockSpec(memory_space=pltpu.SMEM)
    refined = pl.pallas_call(
        functools.partial(kernel, n, cap, cols, slots),
        out_shape=jax.ShapeDtypeStruct(flat, kind),
        in_specs=[vmem, smem, vmem, vmem],
        out_specs=vmem,
        scratch_shapes=[pltpu.SMEM((2 * n, rows, 128), jnp.int32)]
        + [blocks(fetch) for _ in range(10)]
        + [blocks(fetch + 1) for _ in range(4)]
        + [blocks(hold) for _ in range(3)]
        + [
            pltpu.SemaphoreType.DMA((2 * n,)),
            pltpu.SemaphoreType.DMA((2 * n,)),
            pltpu.SemaphoreType.DMA,
            pltpu.SemaphoreType.DMA((4, n)),
            pltpu.SemaphoreType.DMA((4, n)),
            pltpu.SemaphoreType.DMA((4, n)),
            pltpu.SemaphoreType.DMA((4, n)),
        ],
        compiler_params=pltpu.CompilerParams(
            collective_id=0, has_side_effects=True, vmem_limit_bytes=48 * 1024 * 1024
        ),
    )(requests, pairs, s_blocks.reshape(flat), z_blocks.reshape(flat))
    return refined.reshape(z_blocks.shape)


def solution(mesh):
    flat4 = P(("leaf", "col"), None, None, None)
    flat3 = P(("leaf", "col"), None, None)
    asks = P("leaf", "col", None, None)
    in_specs = (flat4, flat4, asks, flat3, asks, flat3, asks, flat3, asks, flat3)
    return jax.shard_map(
        functools.partial(on_device, mesh.shape["col"]),
        mesh=mesh,
        in_specs=in_specs,
        out_specs=flat4,
        check_vma=False,
    )
```

time: 125 us -> 47.6 us (0.38)
  Pallas kernels: 0 us -> 42.7 us
  waiting for transfers between devices: 41.1 us -> 0 us
  starting transfers between devices: 33.8 us -> 0 us
  local copies, waits for them, and re-layouts: 26.6 us -> 4.44 us
  matrix products: 12.5 us -> 0 us
  other arithmetic: 9.53 us -> 0.09 us
    pallas_call x0 -> x1, Pallas kernels: none -> 42.7 us  [on_device(): pl.pallas_call(functools.partial(kernel, n, cap, cols, slots), out_shape=...]
    all_to_all x8 -> x0, waiting for transfers between devices: 33.2 us -> none  [the longest x4 19.6 us: fetch_blocks(): lax.all_to_all(pick_blocks(holdings, lax.all_to_all(requests, 'col', spli...]
    all_to_all x8 -> x0, starting transfers between devices: 30.2 us -> none  [the longest x4 16.6 us: fetch_blocks(): lax.all_to_all(requests, 'col', split_axis=0, concat_axis=0, tiled=True)]
    gather x9 -> x0, local copies, waits for them, and re-layouts: 20.8 us -> none  [the longest x5 18.4 us: block_products(): chosen = jnp.take(padded, lookup, axis=0)]
    dot_general x2 -> x0, matrix products: 12.5 us -> none  [block_products(): jnp.einsum(einsum_form, chosen, local_blocks, preferred_element_type=jnp....]
    ppermute x2 -> x0, waiting for transfers between devices: 7.92 us -> none  [from_partner(): return lax.ppermute(value, axis, pairs)]
    select_n x8 -> x0, other arithmetic: 5.32 us -> none  [the longest x4 3.21 us: pick_blocks(): jnp.where((requests >= 0)[:, :, None, None], blocks, jnp.zeros_like(blocks))]
    all_to_all x4 -> x0, local copies, waits for them, and re-layouts: 5.28 us -> none  [fetch_blocks(): lax.all_to_all(requests, 'col', split_axis=0, concat_axis=0, tiled=True)]
  transfers between devices with their start and end apart: 10 -> 0, of which waited for: 8 -> 0; matrix products, arithmetic and copies ran while one was open for 19% -> 0% of each run, Pallas kernels for 0% -> 0%
where the time goes in v1:
time: 47.6 us; the launch traced here: 47.3 us
  Pallas kernels  42.7 us (90%)
  local copies, waits for them, and re-layouts  4.44 us (9%)
    pallas_call x1, Pallas kernels, on_device(): pl.pallas_call(functools.partial(kernel, n, cap, cols, slots), out_shape=...  42.7 us
    unnamed x21, local copies, waits for them, and re-layouts  4.1 us

profile of v1, /device:TPU:0, one launch (start us, length us, event | category | flops | bytes accessed | tf_op | source)
XLA Modules:
  0.0 47.3 jit_solution(10708714024384932797)
XLA Ops:
  0.0 0.0 copy-start.2
  0.0 0.0 copy-start.6
  0.0 0.0 copy-start.7
  0.0 0.0 copy-start.8
  0.0 0.0 copy-start.9
  0.0 0.0 copy-start.3
  0.0 0.6 %copy-done.6 = s32[1,1,8,1]{2,3,1,0:T(1,128)S(1)} copy-done((s32[1,1,8,1]{2,3,1,0:T(1,128)S(1)}, s32[1,1,8,1]{2,3,1,0:T(1,128)}, u32[]{:S(2)}) %copy-start.6) | copy-done | bytes 56
  0.7 0.0 copy-done.7
  0.7 0.0 copy-done.8
  0.7 0.0 copy-done.9
  0.7 0.1 pad_add_fusion.1
  0.8 0.0 copy-done.2
  0.8 0.0 copy-start.4
  0.8 0.1 reshape.41
  0.9 0.0 copy-done.3
  0.9 0.0 copy-start.5
  0.9 0.1 reshape.42
  1.0 0.5 %copy-done.4 = s32[2,8,8]{2,1,0:T(8,128)S(1)} copy-done((s32[2,8,8]{2,1,0:T(8,128)S(1)}, s32[2,8,8]{2,1,0:T(8,128)}, u32[]{:S(2)}) %copy-start.4) | copy-done | bytes 536
  1.5 0.1 reshape.43
  1.6 0.0 copy-done.5
  1.6 0.1 reshape.44
  1.7 0.0 copy-start
  1.7 1.0 %copy-done = bf16[2,8,128,128]{3,2,1,0:T(8,128)(2,1)S(1)} copy-done((bf16[2,8,128,128]{3,2,1,0:T(8,128)(2,1)S(1)}, bf16[2,8,128,128]{3,2,1,0:T(8,128)(2,1)}, u32[]{:S(2)}) %copy-start) | copy-done | bytes 524312
  2.8 0.0 copy-start.1
  2.8 1.0 %copy-done.1 = bf16[2,8,128,128]{3,2,1,0:T(8,128)(2,1)S(1)} copy-done((bf16[2,8,128,128]{3,2,1,0:T(8,128)(2,1)S(1)}, bf16[2,8,128,128]{3,2,1,0:T(8,128)(2,1)}, u32[]{:S(2)}) %copy-start.1) | copy-done | bytes 524312
  3.8 42.7 %shard_map.100 = bf16[16,128,128]{2,1,0:T(8,128)(2,1)S(1)} custom-call(s32[1,128]{1,0:T(1,128)S(1)} %pad_bitcast_fusion.req_ref, s32[512]{0:T(512)S(1)} %pad_add_fusion.pairs_ref, bf16[16,128,128]{2,1,0:T(8,128)(2,1)S(1)} %bitcast.10, bf16[16,128,128]{2,1,0:T(8,128)(2,1)S(1)} %bitcast.11), custom_call_target="tpu_custom_call" | custom-call | tf_op jit(solution)/shard_map/pallas_call | solution.py:263
  46.5 0.8 %copy.12 = bf16[2,8,128,128]{3,2,1,0:T(8,128)(2,1)} copy(bf16[2,8,128,128]{3,2,1,0:T(8,128)(2,1)S(1)} %bitcast.9) | data formatting | bytes 1048576
  (2 shorter events, 0.0 us)
Async XLA Ops:
  0.0 0.8 %copy-start.2 = (s32[2,8,8]{2,1,0:T(8,128)S(1)}, s32[2,8,8]{2,1,0:T(8,128)}, u32[]{:S(2)}) copy-start(s32[2,8,8]{2,1,0:T(8,128)} %param.13) | copy-start | bytes 1540
  0.0 0.7 %copy-start.6 = (s32[1,1,8,1]{2,3,1,0:T(1,128)S(1)}, s32[1,1,8,1]{2,3,1,0:T(1,128)}, u32[]{:S(2)}) copy-start(s32[1,1,8,1]{2,3,1,0:T(1,128)} %param.16) | copy-start | bytes 100
  0.0 0.7 %copy-start.7 = (s32[1,1,8,1]{2,3,1,0:T(1,128)S(1)}, s32[1,1,8,1]{2,3,1,0:T(1,128)}, u32[]{:S(2)}) copy-start(s32[1,1,8,1]{2,3,1,0:T(1,128)} %param.18) | copy-start | bytes 100
  0.0 0.7 %copy-start.8 = (s32[1,1,8,1]{2,3,1,0:T(1,128)S(1)}, s32[1,1,8,1]{2,3,1,0:T(1,128)}, u32[]{:S(2)}) copy-start(s32[1,1,8,1]{2,3,1,0:T(1,128)} %param.14) | copy-start | bytes 100
  0.0 0.7 %copy-start.9 = (s32[1,1,8,1]{2,3,1,0:T(1,128)S(1)}, s32[1,1,8,1]{2,3,1,0:T(1,128)}, u32[]{:S(2)}) copy-start(s32[1,1,8,1]{2,3,1,0:T(1,128)} %param.12) | copy-start | bytes 100
  0.0 0.9 %copy-start.3 = (s32[2,8,8]{2,1,0:T(8,128)S(1)}, s32[2,8,8]{2,1,0:T(8,128)}, u32[]{:S(2)}) copy-start(s32[2,8,8]{2,1,0:T(8,128)} %param.15) | copy-start | bytes 1540
  0.8 0.7 %copy-start.4 = (s32[2,8,8]{2,1,0:T(8,128)S(1)}, s32[2,8,8]{2,1,0:T(8,128)}, u32[]{:S(2)}) copy-start(s32[2,8,8]{2,1,0:T(8,128)} %param.17) | copy-start | bytes 1540
  0.9 0.7 %copy-start.5 = (s32[2,8,8]{2,1,0:T(8,128)S(1)}, s32[2,8,8]{2,1,0:T(8,128)}, u32[]{:S(2)}) copy-start(s32[2,8,8]{2,1,0:T(8,128)} %param.19) | copy-start | bytes 1540
  1.7 1.0 %copy-start = (bf16[2,8,128,128]{3,2,1,0:T(8,128)(2,1)S(1)}, bf16[2,8,128,128]{3,2,1,0:T(8,128)(2,1)}, u32[]{:S(2)}) copy-start(bf16[2,8,128,128]{3,2,1,0:T(8,128)(2,1)} %param.10) | copy-start | bytes 1572868
  2.8 1.0 %copy-start.1 = (bf16[2,8,128,128]{3,2,1,0:T(8,128)(2,1)S(1)}, bf16[2,8,128,128]{3,2,1,0:T(8,128)(2,1)}, u32[]{:S(2)}) copy-start(bf16[2,8,128,128]{3,2,1,0:T(8,128)(2,1)} %param.11) | copy-start | bytes 1572868

commit v2 on v1

--- a/solution.py
+++ b/solution.py
@@ -16,12 +16,26 @@
     cap,
     cols,
     slots,
+    s_asks,
+    t_asks,
+    z_asks,
+    d_asks,
+    y_names,
+    d_names,
+    e_names,
+    z_names,
+    s_hbm,
+    z_hbm,
+    out_hbm,
     req_ref,
-    pairs_ref,
+    allreq,
+    y_pairs,
+    d_pairs,
+    e_pairs,
+    z_pairs,
     s_ref,
     z_ref,
     out_ref,
-    allreq,
     send_s,
     send_t,
     send_z,
@@ -42,6 +56,8 @@
     req_send,
     req_recv,
     own_sem,
+    in_sem,
+    out_sem,
     z_send,
     z_recv,
     x_send,
@@ -53,6 +69,12 @@
     hold = cols * slots
     size = z_ref.shape[1]
     fetch = n * cap
+    pairs = {S: y_pairs, T: d_pairs, D: e_pairs, Z: z_pairs}
+    asks = (s_asks, t_asks, z_asks, d_asks)
+    moves = [(a, req_ref.at[pl.ds(kind, 1)]) for kind, a in enumerate(asks)]
+    moves += [(s_hbm, s_ref), (z_hbm, z_ref)]
+    moves += [(y_names, y_pairs), (d_names, d_pairs), (e_names, e_pairs), (z_names, z_pairs)]
+    loads = [pltpu.make_async_copy(a, b, in_sem.at[i]) for i, (a, b) in enumerate(moves)]
     sends = {S: send_s, T: send_t, Z: send_z, D: send_d}
     fetched = {S: f_s, T: f_t, Z: f_z, D: f_d}
     xsends = {T: xs_t, Z: xs_z, D: xs_d}
@@ -66,7 +88,14 @@
         lax.fori_loop(0, count, step, 0)
 
     def at(k):
-        return lax.rem(me + k, n)
+        if n & (n - 1):
+            return lax.rem(me + k, n)
+        mask = lax.rem(jnp.int32(n) - k, n)
+        total, bit = 0, 1
+        while bit < n:
+            total += lax.rem(lax.div(me, bit) + lax.div(mask, bit), 2) * bit
+            bit *= 2
+        return total
 
     barrier = pltpu.get_barrier_semaphore()
 
@@ -78,9 +107,13 @@
 
     loop(n - 1, greet_own)
     loop(n, greet_other)
+    for load in loads:
+        load.start()
     for f in (f_s, f_t, f_z, f_d):
         f[fetch] = jnp.zeros((size, size), f.dtype)
     own_copy = pltpu.make_async_copy(req_ref, allreq.at[me], own_sem)
+    for load in loads[:4]:
+        load.wait()
     own_copy.start()
     pl.semaphore_wait(barrier, 2 * n - 1)
 
@@ -97,12 +130,11 @@
     loop(n - 1, lambda k: req_copy(0, leaf, at(k + 1), me).start())
     loop(n, lambda k: req_copy(1, partner, at(k), me).start())
     own_copy.wait()
-    loop(n - 1, lambda k: req_copy(0, leaf, at(k + 1), at(k + 1)).wait_recv())
-    loop(n, lambda k: req_copy(1, partner, at(k), at(k)).wait_recv())
+    for load in loads[4:]:
+        load.wait()
 
     def ask(kind, side, c, q):
-        word = kind * fetch + me * cap + q
-        return allreq[side * n + c, lax.div(word, 128), lax.rem(word, 128)]
+        return allreq[side * n + c, kind, me * cap + q]
 
     def x_copy(kind, c):
         span = pl.ds(c * cap, cap)
@@ -128,6 +160,8 @@
     def x_pass(kind, own_ref):
         def body(k):
             c = at(k)
+            if kind == T:
+                req_copy(1, partner, c, c).wait_recv()
             for q in range(cap):
                 slot = jnp.clip(ask(kind, 1, c, q) - hold, 0, hold - 1)
                 xsends[kind][c * cap + q] = own_ref[slot]
@@ -147,7 +181,9 @@
     def z_pass(kind, own_ref):
         def body(k):
             c = at(k + 1)
-            if kind != S:
+            if kind == S:
+                req_copy(0, leaf, c, c).wait_recv()
+            else:
                 x_copy(kind, c).wait_recv()
             for q in range(cap):
                 sends[kind][c * cap + q] = chosen(kind, own_ref, c, q)
@@ -165,21 +201,22 @@
     def x_order(k):
         return lax.rem(k + 1, n)
 
-    def product(kind, base, local_ref, finish):
+    def product(kind, local_ref, finish, close=None):
         f = fetched[kind]
 
-        def body(a):
-            for g in range(cols):
-                row = base * cols * slots * slots + (g * slots + a) * slots
+        def body(g):
+            rhs = local_ref[pl.ds(g * slots, slots)].reshape(slots * size, size)
+            for a in range(slots):
                 blocks = []
                 for b in range(slots):
-                    name = pairs_ref[row + b]
+                    name = pairs[kind][g, a, b]
                     blocks.append(f[jnp.where(name < 0, fetch, name)])
                 lhs = jnp.concatenate(blocks, axis=1)
-                rhs = local_ref[pl.ds(g * slots, slots)].reshape(slots * size, size)
                 finish(g * slots + a, a, jnp.dot(lhs, rhs, preferred_element_type=jnp.float32))
-
-        loop(slots, body)
+            if close is not None:
+                close(g)
+
+        lax.fori_loop(0, cols, lambda g, c: (body(g), c)[1], 0, unroll=True)
 
     def x_start(kind, own_ref):
         body = x_pass(kind, own_ref)
@@ -195,17 +232,17 @@
     def y_finish(i, a, total):
         y_ref[i] = total.astype(y_ref.dtype)
 
-    product(S, 0, z_ref, y_finish)
+    product(S, z_ref, y_finish)
     z_pass(Z, z_ref)
     arrived(T)
 
     def d_finish(i, a, total):
         rows = lax.broadcasted_iota(jnp.int32, (size, size), 0)
         columns = lax.broadcasted_iota(jnp.int32, (size, size), 1)
-        first = jnp.where(a == 0, 1.0, 0.0)
+        first = 1.0 if a == 0 else 0.0
         d_ref[i] = (jnp.where(rows == columns, first, 0.0) - total).astype(d_ref.dtype)
 
-    product(T, 1, y_ref, d_finish)
+    product(T, y_ref, d_finish)
     x_start(D, d_ref)
     z_pass(D, d_ref)
     arrived(D)
@@ -213,13 +250,18 @@
     def e_finish(i, a, total):
         e_ref[i] = (0.5 * d_ref[i].astype(jnp.float32) + 0.375 * total).astype(e_ref.dtype)
 
-    product(D, 2, d_ref, e_finish)
+    product(D, d_ref, e_finish)
     arrived(Z)
 
     def z_finish(i, a, total):
         out_ref[i] = (z_ref[i].astype(jnp.float32) + total).astype(out_ref.dtype)
 
-    product(Z, 3, e_ref, z_finish)
+    def out_copy(g):
+        span = pl.ds(g * slots, slots)
+        return pltpu.make_async_copy(out_ref.at[span], out_hbm.at[span], out_sem.at[g])
+
+    product(Z, e_ref, z_finish, lambda g: out_copy(g).start())
+    loop(cols, lambda g: out_copy(g).wait())
 
     loop(n - 1, lambda k: req_copy(0, leaf, at(k + 1), me).wait_send())
     loop(n, lambda k: req_copy(1, partner, at(k), me).wait_send())
@@ -247,25 +289,27 @@
     hold = cols * slots
     flat = (hold, size, size)
     fetch = n * cap
-    requests = jnp.concatenate(
-        [r.reshape(-1) for r in (s_requests, zt_requests, z_requests, d_requests)]
-    )
-    rows = pl.cdiv(requests.shape[0], 128)
-    requests = jnp.pad(requests, (0, rows * 128 - requests.shape[0])).reshape(rows, 128)
-    pairs = jnp.concatenate([p.reshape(-1) for p in (y_pairs, d_pairs, e_pairs, z_pairs)])
+    asks = [
+        r.reshape(1, fetch) for r in (s_requests, zt_requests, z_requests, d_requests)
+    ]
+    names = [y_pairs, d_pairs, e_pairs, z_pairs]
     kind = z_blocks.dtype
 
     def blocks(count):
         return pltpu.VMEM((count, size, size), kind)
 
-    vmem = pl.BlockSpec(memory_space=pltpu.VMEM)
-    smem = pl.BlockSpec(memory_space=pltpu.SMEM)
+    hbm = pl.BlockSpec(memory_space=pltpu.HBM)
     refined = pl.pallas_call(
         functools.partial(kernel, n, cap, cols, slots),
         out_shape=jax.ShapeDtypeStruct(flat, kind),
-        in_specs=[vmem, smem, vmem, vmem],
-        out_specs=vmem,
-        scratch_shapes=[pltpu.SMEM((2 * n, rows, 128), jnp.int32)]
+        in_specs=[hbm] * 10,
+        out_specs=hbm,
+        scratch_shapes=[
+            pltpu.SMEM((4, fetch), jnp.int32),
+            pltpu.SMEM((2 * n, 4, fetch), jnp.int32),
+        ]
+        + [pltpu.SMEM(y_pairs.shape, jnp.int32) for _ in range(4)]
+        + [blocks(hold) for _ in range(3)]
         + [blocks(fetch) for _ in range(10)]
         + [blocks(fetch + 1) for _ in range(4)]
         + [blocks(hold) for _ in range(3)]
@@ -273,15 +317,17 @@
             pltpu.SemaphoreType.DMA((2 * n,)),
             pltpu.SemaphoreType.DMA((2 * n,)),
             pltpu.SemaphoreType.DMA,
+            pltpu.SemaphoreType.DMA((10,)),
+            pltpu.SemaphoreType.DMA((cols,)),
             pltpu.SemaphoreType.DMA((4, n)),
             pltpu.SemaphoreType.DMA((4, n)),
             pltpu.SemaphoreType.DMA((4, n)),
             pltpu.SemaphoreType.DMA((4, n)),
         ],
         compiler_params=pltpu.CompilerParams(
-            collective_id=0, has_side_effects=True, vmem_limit_bytes=48 * 1024 * 1024
+            collective_id=0, has_side_effects=True, vmem_limit_bytes=67043328
         ),
-    )(requests, pairs, s_blocks.reshape(flat), z_blocks.reshape(flat))
+    )(*asks, *names, s_blocks.reshape(flat), z_blocks.reshape(flat))
     return refined.reshape(z_blocks.shape)
 
 

time: 47.6 us -> 41.8 us (0.88)
  Pallas kernels: 42.7 us -> 39.7 us
  local copies, waits for them, and re-layouts: 4.44 us -> 1.89 us
    pallas_call x1, Pallas kernels: 42.7 us -> 39.7 us  [on_device(): pl.pallas_call(functools.partial(kernel, n, cap, cols, slots), out_shape=...]
    unnamed x21 -> x1, local copies, waits for them, and re-layouts: 4.1 us -> 1.89 us
where the time goes in v2:
time: 41.8 us; the launch traced here: 41.6 us
  Pallas kernels  39.7 us (95%)
  local copies, waits for them, and re-layouts  1.89 us (5%)
    pallas_call x1, Pallas kernels, on_device(): pl.pallas_call(functools.partial(kernel, n, cap, cols, slots), out_shape=...  39.7 us
    unnamed x1, local copies, waits for them, and re-layouts  1.89 us

profile of v2, /device:TPU:0, one launch (start us, length us, event | category | flops | bytes accessed | tf_op | source)
XLA Modules:
  0.0 41.6 jit_solution(9804606132829034150)
XLA Ops:
  0.0 39.7 %shard_map.100 = bf16[16,128,128]{2,1,0:T(8,128)(2,1)} custom-call(s32[1,8]{1,0:T(1,128)} %bitcast.10, s32[1,8]{1,0:T(1,128)} %bitcast.11, s32[1,8]{1,0:T(1,128)} %bitcast.12, s32[1,8]{1,0:T(1,128)} %bitcast.13, s32[2,8,8]{2,1,0:T(8,128)} %y_names.1, s32[2,8,8]{2,1,0:T(8,128)} %d_names.1, s32[2,8,8]{2,1,0:T(8,128)} %e_names.1, s32[2,8,8]{2,1,0:T(8,128)} %z_names.1, ...), custom_call_target="tpu_custom_call" | custom-call | tf_op jit(solution)/shard_map/pallas_call | solution.py:302
  39.7 1.9 %copy.12 = bf16[2,8,128,128]{3,2,1,0:T(8,128)(2,1)} copy(bf16[2,8,128,128]{3,2,1,0:T(8,128)(2,1)} %bitcast.7) | data formatting | bytes 1048576

commit v3 on v2

--- a/solution.py
+++ b/solution.py
@@ -26,7 +26,7 @@
     z_names,
     s_hbm,
     z_hbm,
-    out_hbm,
+    out_ref,
     req_ref,
     allreq,
     y_pairs,
@@ -35,7 +35,6 @@
     z_pairs,
     s_ref,
     z_ref,
-    out_ref,
     send_s,
     send_t,
     send_z,
@@ -57,7 +56,6 @@
     req_recv,
     own_sem,
     in_sem,
-    out_sem,
     z_send,
     z_recv,
     x_send,
@@ -256,12 +254,7 @@
     def z_finish(i, a, total):
         out_ref[i] = (z_ref[i].astype(jnp.float32) + total).astype(out_ref.dtype)
 
-    def out_copy(g):
-        span = pl.ds(g * slots, slots)
-        return pltpu.make_async_copy(out_ref.at[span], out_hbm.at[span], out_sem.at[g])
-
-    product(Z, e_ref, z_finish, lambda g: out_copy(g).start())
-    loop(cols, lambda g: out_copy(g).wait())
+    product(Z, e_ref, z_finish)
 
     loop(n - 1, lambda k: req_copy(0, leaf, at(k + 1), me).wait_send())
     loop(n, lambda k: req_copy(1, partner, at(k), me).wait_send())
@@ -301,15 +294,15 @@
     hbm = pl.BlockSpec(memory_space=pltpu.HBM)
     refined = pl.pallas_call(
         functools.partial(kernel, n, cap, cols, slots),
-        out_shape=jax.ShapeDtypeStruct(flat, kind),
+        out_shape=pltpu.VMEM(flat, kind),
         in_specs=[hbm] * 10,
-        out_specs=hbm,
+        out_specs=pl.BlockSpec(memory_space=pltpu.VMEM),
         scratch_shapes=[
             pltpu.SMEM((4, fetch), jnp.int32),
             pltpu.SMEM((2 * n, 4, fetch), jnp.int32),
         ]
         + [pltpu.SMEM(y_pairs.shape, jnp.int32) for _ in range(4)]
-        + [blocks(hold) for _ in range(3)]
+        + [blocks(hold) for _ in range(2)]
         + [blocks(fetch) for _ in range(10)]
         + [blocks(fetch + 1) for _ in range(4)]
         + [blocks(hold) for _ in range(3)]
@@ -318,14 +311,13 @@
             pltpu.SemaphoreType.DMA((2 * n,)),
             pltpu.SemaphoreType.DMA,
             pltpu.SemaphoreType.DMA((10,)),
-            pltpu.SemaphoreType.DMA((cols,)),
             pltpu.SemaphoreType.DMA((4, n)),
             pltpu.SemaphoreType.DMA((4, n)),
             pltpu.SemaphoreType.DMA((4, n)),
             pltpu.SemaphoreType.DMA((4, n)),
         ],
         compiler_params=pltpu.CompilerParams(
-            collective_id=0, has_side_effects=True, vmem_limit_bytes=67043328
+            collective_id=0, has_side_effects=True, vmem_limit_bytes=66326528
         ),
     )(*asks, *names, s_blocks.reshape(flat), z_blocks.reshape(flat))
     return refined.reshape(z_blocks.shape)

time: 41.8 us -> 40 us (0.957)
  local copies, waits for them, and re-layouts: 1.89 us -> 0.8 us
  Pallas kernels: 39.7 us -> 39 us
    unnamed x1, local copies, waits for them, and re-layouts: 1.89 us -> 0.8 us
    pallas_call x1, Pallas kernels: 39.7 us -> 39 us  [on_device(): pl.pallas_call(functools.partial(kernel, n, cap, cols, slots), out_shape=...]
where the time goes in v3:
time: 40 us; the launch traced here: 39.8 us
  Pallas kernels  39 us (98%)
  local copies, waits for them, and re-layouts  0.8 us (2%)
    pallas_call x1, Pallas kernels, on_device(): pl.pallas_call(functools.partial(kernel, n, cap, cols, slots), out_shape=...  39 us

profile of v3, /device:TPU:0, one launch (start us, length us, event | category | flops | bytes accessed | tf_op | source)
XLA Modules:
  0.0 39.8 jit_solution(263063895027064857)
XLA Ops:
  0.0 39.0 %shard_map.100 = bf16[16,128,128]{2,1,0:T(8,128)(2,1)S(1)} custom-call(s32[1,8]{1,0:T(1,128)} %bitcast.10, s32[1,8]{1,0:T(1,128)} %bitcast.11, s32[1,8]{1,0:T(1,128)} %bitcast.12, s32[1,8]{1,0:T(1,128)} %bitcast.13, s32[2,8,8]{2,1,0:T(8,128)} %y_names.1, s32[2,8,8]{2,1,0:T(8,128)} %d_names.1, s32[2,8,8]{2,1,0:T(8,128)} %e_names.1, s32[2,8,8]{2,1,0:T(8,128)} %z_names.1, ...), custom_call_target="tpu_custom_call" | custom-call | tf_op jit(solution)/shard_map/pallas_call | solution.py:295
  39.0 0.8 %copy.12 = bf16[2,8,128,128]{3,2,1,0:T(8,128)(2,1)} copy(bf16[2,8,128,128]{3,2,1,0:T(8,128)(2,1)S(1)} %bitcast.7) | data formatting | bytes 1048576

commit v4 on v3

--- a/solution.py
+++ b/solution.py
@@ -83,7 +83,7 @@
             body(k)
             return carry
 
-        lax.fori_loop(0, count, step, 0)
+        lax.fori_loop(0, count, step, 0, unroll=n <= 8)
 
     def at(k):
         if n & (n - 1):
@@ -128,7 +128,7 @@
     loop(n - 1, lambda k: req_copy(0, leaf, at(k + 1), me).start())
     loop(n, lambda k: req_copy(1, partner, at(k), me).start())
     own_copy.wait()
-    for load in loads[4:]:
+    for load in loads[4:6]:
         load.wait()
 
     def ask(kind, side, c, q):
@@ -225,6 +225,8 @@
     x_start(Z, z_ref)
     z_pass(T, z_ref)
 
+    for load in loads[6:]:
+        load.wait()
     arrived(S)
 
     def y_finish(i, a, total):

time: 40 us -> 38.7 us (0.968)
  Pallas kernels: 39 us -> 37.7 us
    pallas_call x1, Pallas kernels: 39 us -> 37.7 us  [on_device(): pl.pallas_call(functools.partial(kernel, n, cap, cols, slots), out_shape=...]
where the time goes in v4:
time: 38.7 us; the launch traced here: 38.5 us
  Pallas kernels  37.7 us (97%)
  local copies, waits for them, and re-layouts  0.8 us (2%)
    pallas_call x1, Pallas kernels, on_device(): pl.pallas_call(functools.partial(kernel, n, cap, cols, slots), out_shape=...  37.7 us
    unnamed x1, local copies, waits for them, and re-layouts  0.8 us

profile of v4, /device:TPU:0, one launch (start us, length us, event | category | flops | bytes accessed | tf_op | source)
XLA Modules:
  0.0 38.5 jit_solution(9520731450567957956)
XLA Ops:
  0.0 37.7 %shard_map.100 = bf16[16,128,128]{2,1,0:T(8,128)(2,1)S(1)} custom-call(s32[1,8]{1,0:T(1,128)} %bitcast.10, s32[1,8]{1,0:T(1,128)} %bitcast.11, s32[1,8]{1,0:T(1,128)} %bitcast.12, s32[1,8]{1,0:T(1,128)} %bitcast.13, s32[2,8,8]{2,1,0:T(8,128)} %y_names.1, s32[2,8,8]{2,1,0:T(8,128)} %d_names.1, s32[2,8,8]{2,1,0:T(8,128)} %e_names.1, s32[2,8,8]{2,1,0:T(8,128)} %z_names.1, ...), custom_call_target="tpu_custom_call" | custom-call | tf_op jit(solution)/shard_map/pallas_call | solution.py:297
  37.7 0.8 %copy.12 = bf16[2,8,128,128]{3,2,1,0:T(8,128)(2,1)} copy(bf16[2,8,128,128]{3,2,1,0:T(8,128)(2,1)S(1)} %bitcast.7) | data formatting | bytes 1048576
